TPU v7x, 32 devices: a whole 2x2x4 slice. The times are simulated.
32 devices in a mesh: tm: 16 (over z, y, x), mp: 2 (over core).
Axes of the slice: x: 2, y: 2, z: 4, core: 2. Of those that a mesh axis runs over, the one named last changes fastest.
Arguments:
- filterbank: bfloat16 [4, 16384, 80], P(None, 'tm'), may hold values from -6 to 6
- lengths: int32 [4], replicated, may hold values from 2048 to 4096, as said below
- bank_begin: int32 [4, 1024], P(None, 'tm'), may hold values from 0 to 1023, as said below
- memory_in: bfloat16 [4, 1024, 1024], P(None, 'tm', 'mp'), may hold values from -6 to 6
- w_front: bfloat16 [320, 1024], P(None, 'mp'), may hold values from -0.3125 to 0.3125
- gain_attn: float32 [1024], replicated, may hold values from 0.25 to 1.75
- w_query: bfloat16 [1024, 1024], P(None, 'mp'), may hold values from -0.1875 to 0.1875
- w_key: bfloat16 [1024, 1024], P(None, 'mp'), may hold values from -0.1875 to 0.1875
- w_value: bfloat16 [1024, 1024], P(None, 'mp'), may hold values from -0.1875 to 0.1875
- w_out: bfloat16 [1024, 1024], P('mp'), may hold values from -0.1875 to 0.1875
- gain_ffn: float32 [1024], replicated, may hold values from 0.25 to 1.75
- w_up: bfloat16 [1024, 4096], P(None, 'mp'), may hold values from -0.1875 to 0.1875
- w_down: bfloat16 [4096, 1024], P('mp'), may hold values from -0.09375 to 0.09375
Outputs:
- encoded: bfloat16 [4, 4096, 1024], P(None, 'tm', 'mp')
- memory_out: bfloat16 [4, 1024, 1024], P(None, 'tm', 'mp')
Inputs may be any that keep to these rules, and one draw needn't show every extreme that they name: `lengths`: some utterance has all 4096 frames. For segment i: max(0, i - 32) <= bank_begin <= max(0, i - 16); in each utterance some segment has bank_begin = i - 32.
All inputs are finite; a program needn't handle non-finite values.
Results may differ from a plain program's by a relative error of at most 0.012.
Values may be sent and summed in bfloat16 or wider, within the bound.
A program may use at most 128 MiB of HBM per device.

v0:
```python
import jax
import jax.numpy as jnp
from jax import lax
from jax.sharding import PartitionSpec as P

HEAD_DIM = 64
STACK = 4
SEG = 4
LC = 32
RC = 4
M = 32
epsilon = 1e-05


def from_behind(block, axis, distance):
    devices = range(lax.axis_size(axis))
    route = [(i - distance, i) for i in devices if i - distance in devices]
    return lax.ppermute(block, axis, route)


def normalize(values, gain):
    center = jnp.mean(values, axis=-1, keepdims=True)
    shifted = values - center
    spread = jnp.mean(shifted * shifted, axis=-1, keepdims=True)
    return shifted * lax.rsqrt(spread + epsilon) * gain


def product(inputs, weight):
    flat_rows = inputs.reshape(-1, inputs.shape[-1])
    result = jnp.dot(flat_rows, weight, preferred_element_type=jnp.float32)
    return result.reshape(inputs.shape[:-1] + (weight.shape[1],))


def rounded(values):
    return lax.optimization_barrier(values.astype(jnp.bfloat16)).astype(jnp.float32)


def body(
    filterbank,
    lengths,
    bank_begin,
    memory_in,
    w_front,
    gain_attn,
    w_query,
    w_key,
    w_value,
    w_out,
    gain_ffn,
    w_up,
    w_down,
):
    batch_count = filterbank.shape[0]
    frames_dev = filterbank.shape[1] // STACK
    segs_dev = frames_dev // SEG
    full_width = w_query.shape[0]
    part_width = w_query.shape[1]
    head_count = part_width // HEAD_DIM
    half_width = full_width // lax.axis_size("mp")
    device_index = lax.axis_index("tm")
    model_index = lax.axis_index("mp")
    column_start = model_index * half_width
    first_frame = device_index * frames_dev
    frame_pos = first_frame + jnp.arange(frames_dev, dtype=jnp.int32)
    valid_frame = frame_pos[None, :] < lengths[:, None]
    seg_global = device_index * segs_dev + jnp.arange(segs_dev, dtype=jnp.int32)
    valid_seg = seg_global[None, :] * SEG < lengths[:, None]
    stacked = filterbank.reshape(batch_count, frames_dev, STACK * filterbank.shape[2])
    front_half = jnp.where(valid_frame[:, :, None], product(stacked, w_front), 0.0).astype(
        jnp.bfloat16
    )
    inputs, memory_full = (
        lax.all_gather(front_half, "mp", axis=2, tiled=True),
        lax.all_gather(memory_in, "mp", axis=2, tiled=True),
    )
    inputs_f = inputs.astype(jnp.float32)
    summary = jnp.mean(inputs_f.reshape(batch_count, segs_dev, SEG, full_width), axis=2)
    normed_all = jnp.concatenate(
        [
            normalize(inputs_f, gain_attn),
            normalize(summary, gain_attn),
            normalize(memory_full.astype(jnp.float32), gain_attn),
        ],
        axis=1,
    ).astype(jnp.bfloat16)
    query_rows = product(normed_all[:, : frames_dev + segs_dev], w_query).astype(jnp.bfloat16)
    key_input = jnp.concatenate(
        [normed_all[:, :frames_dev], normed_all[:, frames_dev + segs_dev :]], axis=1
    )
    key_rows = product(key_input, w_key).astype(jnp.bfloat16)
    value_rows = product(key_input, w_value).astype(jnp.bfloat16)
    frame_keys = key_rows[:, :frames_dev]
    frame_values = value_rows[:, :frames_dev]
    bank_pair = jnp.stack([key_rows[:, frames_dev:], value_rows[:, frames_dev:]])
    left_pair = from_behind(
        jnp.stack([frame_keys[:, frames_dev - LC :], frame_values[:, frames_dev - LC :]]), "tm", 1
    )
    right_pair = from_behind(jnp.stack([frame_keys[:, :RC], frame_values[:, :RC]]), "tm", -1)
    hop_count = -(-M // segs_dev)
    gathered = []
    moving = bank_pair
    moving = from_behind(moving, "tm", 1)
    gathered.insert(0, moving)
    bank_all = jnp.concatenate(gathered + [bank_pair], axis=2)
    all_keys = jnp.concatenate([left_pair[0], frame_keys, right_pair[0], bank_all[0]], axis=1)
    all_values = jnp.concatenate([left_pair[1], frame_values, right_pair[1], bank_all[1]], axis=1)
    query_count = frames_dev + segs_dev
    local_seg = jnp.concatenate(
        [jnp.arange(frames_dev, dtype=jnp.int32) // SEG, jnp.arange(segs_dev, dtype=jnp.int32)]
    )
    query_seg = device_index * segs_dev + local_seg
    bank_floor = jnp.concatenate([jnp.repeat(bank_begin, SEG, axis=1), bank_begin], axis=1)
    key_pos = first_frame - LC + jnp.arange(LC + frames_dev + RC, dtype=jnp.int32)
    key_grid = key_pos[None, None, :]
    seg_grid = query_seg[None, :, None]
    frame_allowed = (
        (key_grid >= seg_grid * SEG - LC)
        & (key_grid < (seg_grid + 1) * SEG + RC)
        & (key_grid >= 0)
        & (key_grid < lengths[:, None, None])
    )
    bank_seg = (device_index - hop_count) * segs_dev + jnp.arange(
        (hop_count + 1) * segs_dev, dtype=jnp.int32
    )
    bank_grid = bank_seg[None, None, :]
    bank_allowed = (bank_grid >= bank_floor[:, :, None]) & (bank_grid <= seg_grid - 1)
    allowed = jnp.concatenate([frame_allowed, bank_allowed], axis=2)
    query_heads = query_rows.reshape(batch_count, query_count, head_count, HEAD_DIM)
    key_heads = all_keys.reshape(batch_count, -1, head_count, HEAD_DIM)
    value_heads = all_values.reshape(batch_count, -1, head_count, HEAD_DIM)
    scores = jnp.einsum(
        "bqhd,bkhd->bhqk", query_heads, key_heads, preferred_element_type=jnp.float32
    ) * HEAD_DIM ** (-0.5)
    weights = jnp.where(allowed[:, None], jnp.exp(scores), 0.0)
    shares = (weights / jnp.sum(weights, axis=-1, keepdims=True)).astype(jnp.bfloat16)
    context = jnp.einsum("bhqk,bkhd->bqhd", shares, value_heads, preferred_element_type=jnp.float32)
    context = context.astype(jnp.bfloat16).reshape(batch_count, query_count, part_width)
    mixed_term = rounded(product(context, w_out))
    frame_term = mixed_term[:, :frames_dev]
    summary_term = mixed_term[:, frames_dev:]
    attention, memory_half = (
        lax.psum_scatter(
            frame_term.astype(jnp.bfloat16), "mp", scatter_dimension=2, tiled=True
        ).astype(jnp.float32),
        lax.psum_scatter(
            summary_term.astype(jnp.bfloat16), "mp", scatter_dimension=2, tiled=True
        ).astype(jnp.float32),
    )
    residual = (front_half.astype(jnp.float32) + attention).astype(jnp.bfloat16)
    residual_f = residual.astype(jnp.float32)
    first_moment, second_moment = lax.psum(
        (jnp.sum(residual_f, axis=-1), jnp.sum(residual_f * residual_f, axis=-1)), "mp"
    )
    center = first_moment / full_width
    spread = second_moment / full_width - center * center
    gain_half = lax.dynamic_slice_in_dim(gain_ffn, column_start, half_width, 0)
    normed_half = (
        (residual_f - center[..., None]) * lax.rsqrt(spread[..., None] + epsilon) * gain_half
    ).astype(jnp.bfloat16)
    normed_ffn = lax.all_gather(normed_half, "mp", axis=2, tiled=True)
    hidden = jax.nn.gelu(product(normed_ffn, w_up)).astype(jnp.bfloat16)
    feed_half = lax.psum_scatter(
        rounded(product(hidden, w_down)).astype(jnp.bfloat16), "mp", scatter_dimension=2, tiled=True
    ).astype(jnp.float32)
    encoded = jnp.where(
        valid_frame[:, :, None], residual.astype(jnp.float32) + feed_half, 0.0
    ).astype(jnp.bfloat16)
    memory_out = jnp.where(valid_seg[:, :, None], memory_half, 0.0).astype(jnp.bfloat16)
    return (encoded, memory_out)


def solution(mesh):
    in_specs = (
        P(None, "tm", None),
        P(),
        P(None, "tm"),
        P(None, "tm", "mp"),
        P(None, "mp"),
        P(),
        P(None, "mp"),
        P(None, "mp"),
        P(None, "mp"),
        P("mp", None),
        P(),
        P(None, "mp"),
        P("mp", None),
    )
    out_specs = (P(None, "tm", "mp"), P(None, "tm", "mp"))
    return jax.shard_map(body, mesh=mesh, in_specs=in_specs, out_specs=out_specs, check_vma=False)
```

profile of v0, /device:TPU:0, one launch (start us, length us, event | category | flops | bytes accessed | tf_op | source)
XLA Modules:
  0.0 166.0 jit_solution(9979901539850414377)
XLA Ops:
  7.3 1.6 copy.25
  8.9 0.7 dot_general.31
  9.6 0.1 broadcast_compare_fusion.2
  9.7 2.6 %select_convert_fusion = bf16[4,256,512]{2,1,0:T(8,128)(2,1)} fusion(bf16[4,256,320]{2,1,0:T(8,128)(2,1)S(1)} %dot_general.31, pred[4,256]{1,0:T(4,128)(4,1)S(1)} %broadcast_compare_fusion.2, bf16[320,512]{1,0:T(8,128)(2,1)} %param.17), kind=kOutput, calls=%fused_computation.55 | convolution fusion | flops 336592896 | bytes 2032640 | tf_op jit(solution)/shard_map/dot_general | solution.py:30
  12.4 2.3 %all_gather.10 = bf16[4,64,1024]{2,1,0:T(8,128)(2,1)S(1)} all-gather(bf16[4,64,512]{2,1,0:T(8,128)(2,1)S(1)} %copy-done.18), channel_id=1, replica_groups=mesh['tm'=16,'mp'=2] {'mp'}, dimensions={2}, use_global_device_ids=true | all-gather | bytes 786432 | tf_op jit(solution)/shard_map/all_gather | solution.py:74
  14.7 0.1 broadcast_in_dim.40
  14.8 0.1 reshape.351
  15.0 0.1 convert_reduce_fusion.2
  15.2 0.1 broadcast_compare_fusion.1
  15.2 0.1 broadcast_compare_fusion
  15.3 0.2 and_and_fusion
  15.5 0.2 compare_and_fusion
  15.7 0.3 broadcast_and_fusion
  16.0 1.1 pad_add_fusion
  17.2 0.3 fusion.66
  17.5 8.4 %all-gather.3.cloned.1.call-done = bf16[4,256,1024]{2,1,0:T(8,128)(2,1)} async-done(((bf16[4,256,512]{2,1,0:T(8,128)(2,1)}), bf16[4,256,1024]{2,1,0:T(8,128)(2,1)}) %all-gather.3.cloned.1.call-update) | async-done | bytes 2097168 | tf_op jit(solution)/shard_map/all_gather | solution.py:73
  25.8 4.8 %reshape.352 = f32[4,64,4,1024]{3,2,1,0:T(4,128)} reshape(bf16[4,256,1024]{2,1,0:T(8,128)(2,1)} %all-gather.3.cloned.1.call-done) | data formatting | bytes 6291456 | tf_op jit(solution)/shard_map/reshape | solution.py:77
  30.6 5.9 %reduce_sum.94 = f32[4,64,1024]{2,1,0:T(8,128)} reduce(f32[4,64,4,1024]{3,2,1,0:T(4,128)} %reshape.352, f32[]{:T(128)} %constant.29.clone.1), dimensions={2}, to_apply=%region_4.5 | reduce | flops 786432 | bytes 5242884 | tf_op jit(solution)/shard_map/reduce_sum | solution.py:77
  36.5 1.4 multiply_reduce_fusion.2
  37.9 1.6 multiply_reduce_fusion.1
  39.5 0.3 convert_reduce_fusion.1
  39.9 0.7 multiply_reduce_fusion
  40.6 0.4 fusion.68
  41.0 0.7 multiply_convert_fusion
  41.7 0.5 copy-done.23
  42.2 1.5 fusion.59
  43.8 1.5 fusion.60
  45.5 0.8 pad_maximum_fusion.8
  46.3 4.5 %collective-permute-start = (bf16[2,4,32,512]{3,2,1,0:T(8,128)(2,1)}, bf16[2,4,32,512]{3,2,1,0:T(8,128)(2,1)}, u32[]{:S(2)}, u32[]{:S(2)}) collective-permute-start(bf16[2,4,32,512]{3,2,1,0:T(8,128)(2,1)} %pad_maximum_fusion.8), channel_id=1, source_target_pairs={{0,2},{2,4},{4,6},{6,8},{8,10},{10,12},{12,14},{14,16},{16,18},{18... | collective-permute-start | bytes 786440 | tf_op jit(solution)/shard_map/ppermute | solution.py:18
  50.8 1.3 collective-permute-start.1
  52.1 0.9 pad_maximum_fusion.7
  52.9 5.3 %collective-permute-start.2 = (bf16[2,4,64,512]{3,2,1,0:T(8,128)(2,1)}, bf16[2,4,64,512]{3,2,1,0:T(8,128)(2,1)}, u32[]{:S(2)}, u32[]{:S(2)}) collective-permute-start(bf16[2,4,64,512]{3,2,1,0:T(8,128)(2,1)} %pad_maximum_fusion.7), channel_id=1, source_target_pairs={{0,2},{2,4},{4,6},{6,8},{8,10},{10,12},{12,14},{14,16},{16,18},{18... | collective-permute-start | bytes 1572872 | tf_op jit(solution)/shard_map/ppermute | solution.py:18
  58.3 2.6 %fusion.61 = bf16[4,320,512]{2,1,0:T(8,128)(2,1)} fusion(bf16[4,64,1024]{2,1,0:T(8,128)(2,1)S(1)} %get-tuple-element.16, bf16[4,256,1024]{2,1,0:T(8,128)(2,1)S(1)} %multiply_convert_fusion, bf16[1024,512]{1,0:T(8,128)(2,1)S(1)} %copy-done.25), kind=kOutput, calls=%fused_computation.63 | convolution fusion | flops 1348075520 | bytes 4980736 | tf_op jit(solution)/shard_map/dot_general | solution.py:30
  60.9 1.2 slice-done.1
  62.1 1.3 copy.32
  63.4 2.6 %copy.31 = bf16[4,320,512]{1,2,0:T(8,128)(2,1)} copy(bf16[4,320,512]{2,1,0:T(8,128)(2,1)} %fusion.61) | data formatting | bytes 2621440 | tf_op jit(solution)/shard_map/convert_element_type | solution.py:86
  66.0 1.3 copy.27
  67.4 1.1 copy.42
  68.5 1.1 copy.40
  69.5 1.0 fusion.86
  70.5 1.0 copy.41
  71.5 1.1 copy.39
  72.6 1.1 maximum_maximum_fusion
  73.7 0.1 fusion.85
  73.8 1.0 copy.33
  74.8 0.3 copy.28
  75.2 12.9 %fusion = (f32[4,8,320]{2,1,0:T(8,128)S(1)}, f32[4,8,320,420]{2,3,1,0:T(8,128)}) fusion(pred[4,320,420]{1,2,0:T(8,128)(4,1)} %pad_add_fusion, bf16[4,320,8,64]{1,3,2,0:T(8,128)(2,1)} %bitcast.57, bf16[4,128,8,64]{1,3,2,0:T(8,128)(2,1)} %bitcast.65, bf16[4,4,8,64]{1,3,2,0:T(8,128)(2,1)} %bitcast.63, bf16[4,256,8,64]{1,3,2,0:T(8,128)(2,1)S(1)} %bitcast.59, ...), kind=kOutput, calls=%fused_computation.2 | convolution fusion | flops 570275840 | bytes 20812800 | tf_op jit(solution)/shard_map/bqhd,bkhd->bhqk/dot_general | solution.py:131
  88.1 10.9 %fusion.54 = bf16[4,8,64,320]{3,2,1,0:T(8,128)(2,1)S(1)} fusion(f32[4,8,320,420]{2,3,1,0:T(8,128)} %get-tuple-element.21, f32[4,8,320]{2,1,0:T(8,128)S(1)} %get-tuple-element.20, pred[4,320,420]{1,2,0:T(8,128)(4,1)S(1)} %copy-done.15, bf16[4,128,8,64]{1,3,2,0:T(8,128)(2,1)S(1)} %bitcast.64, bf16[4,4,8,64]{1,3,2,0:T(8,128)(2,1)S(1)} %bitcast.62, ...), kind=kOutput, calls=%fused_computation.58 | convolution fusion | flops 575242240 | bytes 20812800 | tf_op jit(solution)/shard_map/bhqk,bkhd->bqhd/dot_general | solution.py:136
  99.1 1.6 convolution_convert_fusion
  100.7 1.5 copy-done.8
  102.2 1.5 slice.94
  103.7 0.3 all-gather.5.cloned.1.call-start
  104.0 0.1 dynamic_slice.3
  104.0 9.9 %reduce-scatter.4.cloned.1.call-done = bf16[4,256,512]{2,1,0:T(8,128)(2,1)} async-done(((bf16[4,256,1024]{2,1,0:T(8,128)(2,1)}), bf16[4,256,512]{2,1,0:T(8,128)(2,1)}) %reduce-scatter.4.cloned.1.call-update) | async-done | bytes 1048592 | tf_op jit(solution)/shard_map/reduce_scatter | solution.py:142
  113.9 1.8 %convert_reduce_fusion = (f32[4,256]{1,0:T(4,128)S(1)}, f32[4,256]{1,0:T(4,128)S(1)}, bf16[4,256,512]{2,1,0:T(8,128)(2,1)S(1)}) fusion(bf16[4,256,512]{2,1,0:T(8,128)(2,1)} %reduce-scatter.4.cloned.1.call-done, bf16[4,256,512]{2,1,0:T(8,128)(2,1)S(1)} %copy-done.5), kind=kLoop, calls=%fused_computation.25 | loop fusion | flops 4192256 | bytes 3153920 | tf_op jit(solution)/shard_map/reduce_sum | solution.py:152
  115.7 2.5 %all-reduce = (f32[4,256]{1,0:T(4,128)S(1)}, f32[4,256]{1,0:T(4,128)S(1)}) all-reduce(f32[4,256]{1,0:T(4,128)S(1)} %get-tuple-element.3, f32[4,256]{1,0:T(4,128)S(1)} %get-tuple-element.2), channel_id=1, replica_groups=mesh['tm'=16,'mp'=2] {'mp'}, use_global_device_ids=true, to_apply=%region_12.13 | all-reduce | flops 2048 | bytes 16384 | tf_op jit(solution)/shard_map/psum | solution.py:151
  118.2 1.4 fusion.28
  119.7 1.9 %slice.95 = bf16[4,64,1024]{2,1,0:T(8,128)(2,1)} slice(bf16[4,320,1024]{2,1,0:T(8,128)(2,1)} %copy-done.8), slice={[0:4], [256:320], [0:1024]} | slice | bytes 1048576 | tf_op jit(solution)/shard_map/slice | solution.py:140
  121.6 10.0 %all-gather.5.cloned.1.call-done = bf16[4,256,1024]{2,1,0:T(8,128)(2,1)} async-done(((bf16[4,256,512]{2,1,0:T(8,128)(2,1)}), bf16[4,256,1024]{2,1,0:T(8,128)(2,1)}) %all-gather.5.cloned.1.call-update) | async-done | bytes 2097168 | tf_op jit(solution)/shard_map/all_gather | solution.py:160
  131.6 14.3 %fusion.47 = bf16[4,256,1024]{2,1,0:T(8,128)(2,1)} fusion(bf16[2048,1024]{1,0:T(8,128)(2,1)} %param.25, bf16[4,256,1024]{2,1,0:T(8,128)(2,1)} %all-gather.5.cloned.1.call-done, bf16[1024,2048]{1,0:T(8,128)(2,1)} %param.24), kind=kOutput, calls=%fused_computation.57 | convolution fusion | flops 8609857536 | bytes 12582912 | tf_op jit(solution)/shard_map/dot_general | solution.py:30
  146.0 0.1 broadcast_compare_fusion.3
  146.1 1.8 %select_convert_fusion.1 = bf16[4,64,512]{2,1,0:T(8,128)(2,1)} fusion(bf16[4,64,512]{2,1,0:T(8,128)(2,1)} %reduce-scatter.8.cloned.1.call-done, pred[4,64]{1,0:T(4,128)(4,1)S(1)} %broadcast_compare_fusion.3), kind=kLoop, calls=%fused_computation.82 | loop fusion | flops 393216 | bytes 524544 | tf_op jit(solution)/shard_map/convert_element_type | solution.py:168
  147.8 9.1 %reduce-scatter.6.cloned.1.call-done = bf16[4,256,512]{2,1,0:T(8,128)(2,1)} async-done(((bf16[4,256,1024]{2,1,0:T(8,128)(2,1)}), bf16[4,256,512]{2,1,0:T(8,128)(2,1)}) %reduce-scatter.6.cloned.1.call-update) | async-done | bytes 1048592 | tf_op jit(solution)/shard_map/reduce_scatter | solution.py:162
  156.9 2.5 %fusion.31 = bf16[4,256,512]{2,1,0:T(8,128)(2,1)} fusion(bf16[4,256,512]{2,1,0:T(8,128)(2,1)S(1)} %get-tuple-element.6, bf16[4,256,512]{2,1,0:T(8,128)(2,1)} %reduce-scatter.6.cloned.1.call-done, pred[4,256]{1,0:T(4,128)(4,1)S(1)} %broadcast_compare_fusion.2), kind=kLoop, calls=%fused_computation.38 | loop fusion | flops 2621440 | bytes 3146752 | tf_op jit(solution)/shard_map/convert_element_type | solution.py:167
  (87 shorter events, 0.6 us)
Async XLA Ops:
  7.2 91.9 %copy-start = (bf16[512,1024]{1,0:T(8,128)(2,1)S(1)}, bf16[512,1024]{1,0:T(8,128)(2,1)}, u32[]{:S(2)}) copy-start(bf16[512,1024]{1,0:T(8,128)(2,1)} %param.22) | copy-start | bytes 3145732
  7.2 2.4 %copy-start.21 = (s32[4]{0:T(128)S(1)}, s32[4]{0:T(128)}, u32[]{:S(2)}) copy-start(s32[4]{0:T(128)} %param.14) | copy-start | bytes 52
  7.2 18.6 %all-gather.3.cloned.1.call-start = ((), (), s32[]{:S(2)}) async-start(), calls=%async_computation.3 | async-start | bytes 3145728 | tf_op jit(solution)/shard_map/all_gather | solution.py:73
  8.9 3.5 %copy-start.18 = (bf16[4,64,512]{2,1,0:T(8,128)(2,1)S(1)}, bf16[4,64,512]{2,1,0:T(8,128)(2,1)}, u32[]{:S(2)}) copy-start(bf16[4,64,512]{2,1,0:T(8,128)(2,1)} %param.16) | copy-start | bytes 786436
  9.6 5.2 %copy-start.20 = (s32[4,64]{1,0:T(4,128)S(1)}, s32[4,64]{1,0:T(4,128)}, u32[]{:S(2)}) copy-start(s32[4,64]{1,0:T(4,128)} %param.15) | copy-start | bytes 3076
  12.3 101.6 %reduce-scatter.4.cloned.1.call-start = ((), (), s32[]{:S(2)}) async-start(), calls=%async_computation.4 | async-start | bytes 3145728 | tf_op jit(solution)/shard_map/reduce_scatter | solution.py:142
  14.7 11.1 %copy-start.3 = (bf16[4,64,1024]{2,1,0:T(8,128)(2,1)}, bf16[4,64,1024]{2,1,0:T(8,128)(2,1)S(1)}, u32[]{:S(2)}) copy-start(bf16[4,64,1024]{2,1,0:T(8,128)(2,1)S(1)} %all_gather.10) | copy-start | bytes 1572868
  30.6 9.0 %copy-start.1 = (bf16[4,256,1024]{2,1,0:T(8,128)(2,1)S(1)}, bf16[4,256,1024]{2,1,0:T(8,128)(2,1)}, u32[]{:S(2)}) copy-start(bf16[4,256,1024]{2,1,0:T(8,128)(2,1)} %all-gather.3.cloned.1.call-done) | copy-start | bytes 6291460
  37.9 2.7 %copy-start.2 = (f32[4,64,1024]{2,1,0:T(8,128)S(1)}, f32[4,64,1024]{2,1,0:T(8,128)}, u32[]{:S(2)}) copy-start(f32[4,64,1024]{2,1,0:T(8,128)} %reduce_sum.94) | copy-start | bytes 3145732
  37.9 2.7 %copy-start.4 = (bf16[4,64,1024]{2,1,0:T(8,128)(2,1)S(1)}, bf16[4,64,1024]{2,1,0:T(8,128)(2,1)}, u32[]{:S(2)}) copy-start(bf16[4,64,1024]{2,1,0:T(8,128)(2,1)} %copy-done.3) | copy-start | bytes 1572868
  37.9 2.7 %copy-start.19 = (f32[1024]{0:T(1024)S(1)}, f32[1024]{0:T(1024)}, u32[]{:S(2)}) copy-start(f32[1024]{0:T(1024)} %param.18) | copy-start | bytes 12292
  41.0 1.2 copy-start.23
  42.2 1.5 copy-start.24
  43.8 17.1 %copy-start.7 = (bf16[4,320,512]{2,1,0:T(8,128)(2,1)}, bf16[4,320,512]{2,1,0:T(8,128)(2,1)S(1)}, u32[]{:S(2)}) copy-start(bf16[4,320,512]{2,1,0:T(8,128)(2,1)S(1)} %fusion.59) | copy-start | bytes 3932164
  45.4 15.6 %copy-start.6 = (bf16[4,320,512]{2,1,0:T(8,128)(2,1)}, bf16[4,320,512]{2,1,0:T(8,128)(2,1)S(1)}, u32[]{:S(2)}) copy-start(bf16[4,320,512]{2,1,0:T(8,128)(2,1)S(1)} %fusion.60) | copy-start | bytes 3932164
  45.4 12.9 %copy-start.25 = (bf16[1024,512]{1,0:T(8,128)(2,1)S(1)}, bf16[1024,512]{1,0:T(8,128)(2,1)}, u32[]{:S(2)}) copy-start(bf16[1024,512]{1,0:T(8,128)(2,1)} %param.19) | copy-start | bytes 3145732
  45.5 6.6 %copy-start.9 = (bf16[1,4,64,512]{3,2,1,0:T(8,128)(2,1)}, bf16[1,4,64,512]{3,2,1,0:T(8,128)(2,1)S(1)}, u32[]{:S(2)}) copy-start(bf16[1,4,64,512]{3,2,1,0:T(8,128)(2,1)S(1)} %get-tuple-element.22) | copy-start | bytes 786436
  45.5 7.5 %copy-start.11 = (bf16[1,4,64,512]{3,2,1,0:T(8,128)(2,1)}, bf16[1,4,64,512]{3,2,1,0:T(8,128)(2,1)S(1)}, u32[]{:S(2)}) copy-start(bf16[1,4,64,512]{3,2,1,0:T(8,128)(2,1)S(1)} %get-tuple-element.23) | copy-start | bytes 786436
  46.3 23.3 %collective-permute-start = (bf16[2,4,32,512]{3,2,1,0:T(8,128)(2,1)}, bf16[2,4,32,512]{3,2,1,0:T(8,128)(2,1)}, u32[]{:S(2)}, u32[]{:S(2)}) collective-permute-start(bf16[2,4,32,512]{3,2,1,0:T(8,128)(2,1)} %pad_maximum_fusion.8), channel_id=1, source_target_pairs={{0,2},{2,4},{4,6},{6,8},{8,10},{10,12},{12,14},{14,16},{16,18},{18... | collective-permute-start | bytes 786440 | tf_op jit(solution)/shard_map/ppermute | solution.py:18
  50.8 16.6 %collective-permute-start.1 = (bf16[2,4,4,512]{3,2,1,0:T(4,128)(2,1)S(1)}, bf16[2,4,4,512]{3,2,1,0:T(4,128)(2,1)S(1)}, u32[]{:S(2)}, u32[]{:S(2)}) collective-permute-start(bf16[2,4,4,512]{3,2,1,0:T(4,128)(2,1)S(1)} %pad_maximum_fusion.9), channel_id=1, source_target_pairs={{2,0},{4,2},{6,4},{8,6},{10,8},{12,10},{14,12},{16,14},{18,16},{20... | collective-permute-start | bytes 98312 | tf_op jit(solution)/shard_map/ppermute | solution.py:18
  52.9 19.7 %collective-permute-start.2 = (bf16[2,4,64,512]{3,2,1,0:T(8,128)(2,1)}, bf16[2,4,64,512]{3,2,1,0:T(8,128)(2,1)}, u32[]{:S(2)}, u32[]{:S(2)}) collective-permute-start(bf16[2,4,64,512]{3,2,1,0:T(8,128)(2,1)} %pad_maximum_fusion.7), channel_id=1, source_target_pairs={{0,2},{2,4},{4,6},{6,8},{8,10},{10,12},{12,14},{14,16},{16,18},{18... | collective-permute-start | bytes 1572872 | tf_op jit(solution)/shard_map/ppermute | solution.py:18
  60.9 1.2 slice-start.1
  62.1 3.9 %slice-start = ((bf16[4,320,512]{2,1,0:T(8,128)(2,1)}), bf16[4,256,512]{2,1,0:T(8,128)(2,1)S(1)}, s32[]{:S(2)}) async-start(bf16[4,320,512]{2,1,0:T(8,128)(2,1)} %copy-done.6), calls=%async_computation.8 | async-start | bytes 2097152 | tf_op jit(solution)/shard_map/slice | solution.py:93
  66.0 6.6 %copy-start.10 = (bf16[1,4,64,512]{3,2,1,0:T(8,128)(2,1)S(1)}, bf16[1,4,64,512]{3,2,1,0:T(8,128)(2,1)}, u32[]{:S(2)}) copy-start(bf16[1,4,64,512]{3,2,1,0:T(8,128)(2,1)} %copy-done.9) | copy-start | bytes 786436
  66.0 6.6 %copy-start.12 = (bf16[1,4,64,512]{3,2,1,0:T(8,128)(2,1)S(1)}, bf16[1,4,64,512]{3,2,1,0:T(8,128)(2,1)}, u32[]{:S(2)}) copy-start(bf16[1,4,64,512]{3,2,1,0:T(8,128)(2,1)} %copy-done.11) | copy-start | bytes 786436
  73.7 1.4 copy-start.14
  75.1 13.0 %copy-start.13 = (bf16[4,256,512]{1,2,0:T(8,128)(2,1)S(1)}, bf16[4,256,512]{1,2,0:T(8,128)(2,1)}, u32[]{:S(2)}) copy-start(bf16[4,256,512]{1,2,0:T(8,128)(2,1)} %copy.27) | copy-start | bytes 3145732
  75.1 13.0 %copy-start.15 = (pred[4,320,420]{1,2,0:T(8,128)(4,1)S(1)}, pred[4,320,420]{1,2,0:T(8,128)(4,1)}, u32[]{:S(2)}) copy-start(pred[4,320,420]{1,2,0:T(8,128)(4,1)} %pad_add_fusion) | copy-start | bytes 1612804
  75.1 13.0 %copy-start.16 = (bf16[1,4,32,512]{2,3,1,0:T(8,128)(2,1)S(1)}, bf16[1,4,32,512]{2,3,1,0:T(8,128)(2,1)}, u32[]{:S(2)}) copy-start(bf16[1,4,32,512]{2,3,1,0:T(8,128)(2,1)} %copy.39) | copy-start | bytes 393220
  75.1 13.0 %copy-start.17 = (bf16[1,4,4,512]{2,3,1,0:T(8,128)(2,1)S(1)}, bf16[1,4,4,512]{2,3,1,0:T(8,128)(2,1)}, u32[]{:S(2)}) copy-start(bf16[1,4,4,512]{2,3,1,0:T(8,128)(2,1)} %copy.40) | copy-start | bytes 49156
  100.7 1.5 copy-start.8
  102.2 1.8 %copy-start.22 = (f32[1024]{0:T(1024)S(1)}, f32[1024]{0:T(1024)}, u32[]{:S(2)}) copy-start(f32[1024]{0:T(1024)} %param.23) | copy-start | bytes 12292
  102.2 11.8 %copy-start.5 = (bf16[4,256,512]{2,1,0:T(8,128)(2,1)S(1)}, bf16[4,256,512]{2,1,0:T(8,128)(2,1)}, u32[]{:S(2)}) copy-start(bf16[4,256,512]{2,1,0:T(8,128)(2,1)} %select_convert_fusion) | copy-start | bytes 3145732
  103.7 27.9 %all-gather.5.cloned.1.call-start = ((), (), s32[]{:S(2)}) async-start(), calls=%async_computation.5 | async-start | bytes 3145728 | tf_op jit(solution)/shard_map/all_gather | solution.py:160
  119.6 26.4 %reduce-scatter.8.cloned.1.call-start = ((), (), s32[]{:S(2)}) async-start(), calls=%async_computation.7 | async-start | bytes 786432 | tf_op jit(solution)/shard_map/reduce_scatter | solution.py:145
  121.6 35.3 %reduce-scatter.6.cloned.1.call-start = ((), (), s32[]{:S(2)}) async-start(), calls=%async_computation.6 | async-start | bytes 3145728 | tf_op jit(solution)/shard_map/reduce_scatter | solution.py:162
Sparse Core Ops, SparseCore 0:
  12.5 13.2 all-gather.2
  103.8 10.0 reduce-scatter.3
  119.7 11.8 all-gather.4
  133.7 9.0 reduce-scatter.7
  146.1 10.7 reduce-scatter.5
where the time goes:
time: 167 us; the launch traced here: 166 us
  matrix products  48.1 us (29%)
  waiting for transfers between devices  37.4 us (22%)
  local copies, waits for them, and re-layouts  26 us (16%)
  other arithmetic  23.9 us (14%)
  between operations  14.3 us (9%)
  starting transfers between devices  11.5 us (7%)
  blocking collectives  4.79 us (3%)
    dot_general x6, matrix products, product(): result = jnp.dot(flat_rows, weight, preferred_element_type=jnp.float32)  24.3 us
    dot_general x1, matrix products, body(): jnp.einsum('bqhd,bkhd->bhqk', query_heads, key_heads, preferred_element_t...  12.9 us
    ppermute x3, starting transfers between devices, from_behind(): return lax.ppermute(block, axis, route)  11.1 us
    dot_general x1, matrix products, body(): jnp.einsum('bhqk,bkhd->bqhd', shares, value_heads, preferred_element_type...  10.9 us
    all_gather x1, waiting for transfers between devices, body(): normed_ffn = lax.all_gather(normed_half, 'mp', axis=2, tiled=True)  9.98 us
    reduce_scatter x1, waiting for transfers between devices, body(): lax.psum_scatter(frame_term.astype(jnp.bfloat16), 'mp', scatter_dimension...  9.89 us
    reduce_scatter x1, waiting for transfers between devices, body(): lax.psum_scatter(rounded(product(hidden, w_down)).astype(jnp.bfloat16), '...  9.09 us
    all_gather x1, waiting for transfers between devices, body(): lax.all_gather(front_half, 'mp', axis=2, tiled=True)  8.35 us
  transfers between devices with their start and end apart: 8, of which 4 were waited for; matrix products, arithmetic and copies ran while one was open for 21% of the time, Pallas kernels for 0%

commit v1 on v0

--- a/solution.py
+++ b/solution.py
@@ -157,7 +157,7 @@
     normed_half = (
         (residual_f - center[..., None]) * lax.rsqrt(spread[..., None] + epsilon) * gain_half
     ).astype(jnp.bfloat16)
-    normed_ffn = lax.all_gather(normed_half, "mp", axis=2, tiled=True)
+    normed_ffn = jnp.concatenate(lax.all_gather(normed_half, "mp"), axis=2)
     hidden = jax.nn.gelu(product(normed_ffn, w_up)).astype(jnp.bfloat16)
     feed_half = lax.psum_scatter(
         rounded(product(hidden, w_down)).astype(jnp.bfloat16), "mp", scatter_dimension=2, tiled=True

time: 167 us -> 176 us (1.054)
  local copies, waits for them, and re-layouts: 26 us -> 35.5 us
    all_gather x0 -> x1, local copies, waits for them, and re-layouts: none -> 5.08 us  [body(): normed_ffn = jnp.concatenate(lax.all_gather(normed_half, 'mp'), axis=2)]
    dot_general x1 -> x2, local copies, waits for them, and re-layouts: 0.67 us -> 5.11 us  [product(): result = jnp.dot(flat_rows, weight, preferred_element_type=jnp.float32)]
  transfers between devices with their start and end apart: 8 -> 8, of which waited for: 4 -> 4; matrix products, arithmetic and copies ran while one was open for 21% -> 25% of each run, Pallas kernels for 0% -> 0%
where the time goes in v1:
time: 176 us
  matrix products  48.2 us (27%)
  waiting for transfers between devices  37.4 us (21%)
  local copies, waits for them, and re-layouts  35.5 us (20%)
  other arithmetic  23.9 us (14%)
  between operations  14.3 us (8%)
  starting transfers between devices  11.5 us (7%)
  blocking collectives  4.79 us (3%)
    dot_general x6, matrix products, product(): result = jnp.dot(flat_rows, weight, preferred_element_type=jnp.float32)  24.4 us
    dot_general x1, matrix products, body(): jnp.einsum('bqhd,bkhd->bhqk', query_heads, key_heads, preferred_element_t...  12.9 us
    ppermute x3, starting transfers between devices, from_behind(): return lax.ppermute(block, axis, route)  11.1 us
    dot_general x1, matrix products, body(): jnp.einsum('bhqk,bkhd->bqhd', shares, value_heads, preferred_element_type...  10.9 us
    all_gather x1, waiting for transfers between devices, body(): normed_ffn = jnp.concatenate(lax.all_gather(normed_half, 'mp'), axis=2)  9.98 us
    reduce_scatter x1, waiting for transfers between devices, body(): lax.psum_scatter(frame_term.astype(jnp.bfloat16), 'mp', scatter_dimension...  9.89 us
    reduce_scatter x1, waiting for transfers between devices, body(): lax.psum_scatter(rounded(product(hidden, w_down)).astype(jnp.bfloat16), '...  9.06 us
    all_gather x1, waiting for transfers between devices, body(): lax.all_gather(front_half, 'mp', axis=2, tiled=True)  8.35 us
  transfers between devices with their start and end apart: 8, of which 4 were waited for; matrix products, arithmetic and copies ran while one was open for 25% of the time, Pallas kernels for 0%

profile of v1, /device:TPU:0, one launch (start us, length us, event | category | flops | bytes accessed | tf_op | source)
XLA Modules:
  0.0 175.6 jit_solution(9814731270255909501)
XLA Ops:
  7.3 1.6 copy.39
  8.9 0.7 dot_general.33
  9.6 0.1 broadcast_compare_fusion.2
  9.7 2.6 %select_convert_fusion = bf16[4,256,512]{2,1,0:T(8,128)(2,1)} fusion(bf16[4,256,320]{2,1,0:T(8,128)(2,1)S(1)} %dot_general.33, pred[4,256]{1,0:T(4,128)(4,1)S(1)} %broadcast_compare_fusion.2, bf16[320,512]{1,0:T(8,128)(2,1)} %param.17), kind=kOutput, calls=%fused_computation.56 | convolution fusion | flops 336592896 | bytes 2032640 | tf_op jit(solution)/shard_map/dot_general | solution.py:30
  12.4 2.3 %all_gather.13 = bf16[4,64,1024]{2,1,0:T(8,128)(2,1)S(1)} all-gather(bf16[4,64,512]{2,1,0:T(8,128)(2,1)S(1)} %copy-done.18), channel_id=1, replica_groups=mesh['tm'=16,'mp'=2] {'mp'}, dimensions={2}, use_global_device_ids=true | all-gather | bytes 786432 | tf_op jit(solution)/shard_map/all_gather | solution.py:74
  14.7 0.1 broadcast_in_dim.40
  14.8 0.1 reshape.353
  15.0 0.1 convert_reduce_fusion.2
  15.2 0.1 broadcast_compare_fusion
  15.3 0.2 and_and_fusion
  15.5 0.2 compare_and_fusion
  15.7 0.3 broadcast_and_fusion
  16.0 1.1 pad_add_fusion
  17.2 0.3 fusion.66
  17.5 8.4 %all-gather.4.cloned.1.call-done = bf16[4,256,1024]{2,1,0:T(8,128)(2,1)} async-done(((bf16[4,256,512]{2,1,0:T(8,128)(2,1)}), bf16[4,256,1024]{2,1,0:T(8,128)(2,1)}) %all-gather.4.cloned.1.call-update) | async-done | bytes 2097168 | tf_op jit(solution)/shard_map/all_gather | solution.py:73
  25.8 4.8 %reshape.354 = f32[4,64,4,1024]{3,2,1,0:T(4,128)} reshape(bf16[4,256,1024]{2,1,0:T(8,128)(2,1)} %all-gather.4.cloned.1.call-done) | data formatting | bytes 6291456 | tf_op jit(solution)/shard_map/reshape | solution.py:77
  30.6 5.9 %reduce_sum.94 = f32[4,64,1024]{2,1,0:T(8,128)} reduce(f32[4,64,4,1024]{3,2,1,0:T(4,128)} %reshape.354, f32[]{:T(128)} %constant.29.clone.1), dimensions={2}, to_apply=%region_4.5 | reduce | flops 786432 | bytes 5242884 | tf_op jit(solution)/shard_map/reduce_sum | solution.py:77
  36.5 1.4 multiply_reduce_fusion.2
  37.9 1.6 multiply_reduce_fusion.1
  39.5 0.3 convert_reduce_fusion.1
  39.9 0.7 multiply_reduce_fusion
  40.6 0.4 fusion.68
  41.0 0.7 multiply_convert_fusion
  41.7 0.5 copy-done.23
  42.2 1.5 fusion.59
  43.8 1.5 fusion.60
  45.5 0.8 pad_maximum_fusion.8
  46.3 4.5 %collective-permute-start = (bf16[2,4,32,512]{3,2,1,0:T(8,128)(2,1)}, bf16[2,4,32,512]{3,2,1,0:T(8,128)(2,1)}, u32[]{:S(2)}, u32[]{:S(2)}) collective-permute-start(bf16[2,4,32,512]{3,2,1,0:T(8,128)(2,1)} %pad_maximum_fusion.8), channel_id=1, source_target_pairs={{0,2},{2,4},{4,6},{6,8},{8,10},{10,12},{12,14},{14,16},{16,18},{18... | collective-permute-start | bytes 786440 | tf_op jit(solution)/shard_map/ppermute | solution.py:18
  50.8 1.3 collective-permute-start.1
  52.1 0.9 pad_maximum_fusion.7
  52.9 5.3 %collective-permute-start.2 = (bf16[2,4,64,512]{3,2,1,0:T(8,128)(2,1)}, bf16[2,4,64,512]{3,2,1,0:T(8,128)(2,1)}, u32[]{:S(2)}, u32[]{:S(2)}) collective-permute-start(bf16[2,4,64,512]{3,2,1,0:T(8,128)(2,1)} %pad_maximum_fusion.7), channel_id=1, source_target_pairs={{0,2},{2,4},{4,6},{6,8},{8,10},{10,12},{12,14},{14,16},{16,18},{18... | collective-permute-start | bytes 1572872 | tf_op jit(solution)/shard_map/ppermute | solution.py:18
  58.3 2.6 %fusion.61 = bf16[4,320,512]{2,1,0:T(8,128)(2,1)} fusion(bf16[4,64,1024]{2,1,0:T(8,128)(2,1)S(1)} %get-tuple-element.16, bf16[4,256,1024]{2,1,0:T(8,128)(2,1)S(1)} %multiply_convert_fusion, bf16[1024,512]{1,0:T(8,128)(2,1)S(1)} %copy-done.25), kind=kOutput, calls=%fused_computation.64 | convolution fusion | flops 1348075520 | bytes 4980736 | tf_op jit(solution)/shard_map/dot_general | solution.py:30
  60.9 1.2 slice-done.1
  62.1 1.3 copy.46
  63.4 2.6 %copy.45 = bf16[4,320,512]{1,2,0:T(8,128)(2,1)} copy(bf16[4,320,512]{2,1,0:T(8,128)(2,1)} %fusion.61) | data formatting | bytes 2621440 | tf_op jit(solution)/shard_map/convert_element_type | solution.py:86
  66.0 1.3 copy.41
  67.4 1.1 copy.57
  68.5 1.1 copy.55
  69.5 1.0 fusion.86
  70.5 1.0 copy.56
  71.5 1.1 copy.54
  72.6 1.1 maximum_maximum_fusion
  73.8 1.0 copy.47
  74.8 0.3 copy.42
  75.2 12.9 %fusion = (f32[4,8,320]{2,1,0:T(8,128)S(1)}, f32[4,8,320,420]{2,3,1,0:T(8,128)}) fusion(pred[4,320,420]{1,2,0:T(8,128)(4,1)} %pad_add_fusion, bf16[4,320,8,64]{1,3,2,0:T(8,128)(2,1)} %bitcast.63, bf16[4,128,8,64]{1,3,2,0:T(8,128)(2,1)} %bitcast.71, bf16[4,4,8,64]{1,3,2,0:T(8,128)(2,1)} %bitcast.69, bf16[4,256,8,64]{1,3,2,0:T(8,128)(2,1)S(1)} %bitcast.65, ...), kind=kOutput, calls=%fused_computation.2 | convolution fusion | flops 570275840 | bytes 20812800 | tf_op jit(solution)/shard_map/bqhd,bkhd->bhqk/dot_general | solution.py:131
  88.1 10.9 %fusion.54 = bf16[4,8,64,320]{3,2,1,0:T(8,128)(2,1)S(1)} fusion(f32[4,8,320,420]{2,3,1,0:T(8,128)} %get-tuple-element.21, f32[4,8,320]{2,1,0:T(8,128)S(1)} %get-tuple-element.20, pred[4,320,420]{1,2,0:T(8,128)(4,1)S(1)} %copy-done.15, bf16[4,128,8,64]{1,3,2,0:T(8,128)(2,1)S(1)} %bitcast.70, bf16[4,4,8,64]{1,3,2,0:T(8,128)(2,1)S(1)} %bitcast.68, ...), kind=kOutput, calls=%fused_computation.59 | convolution fusion | flops 575242240 | bytes 20812800 | tf_op jit(solution)/shard_map/bhqk,bkhd->bqhd/dot_general | solution.py:136
  99.1 1.6 convolution_convert_fusion
  100.7 1.5 copy-done.8
  102.2 1.5 slice.94
  103.7 0.3 all-gather.6.cloned.1.call-start
  104.0 0.1 dynamic_slice.3
  104.0 9.9 %reduce-scatter.4.cloned.1.call-done = bf16[4,256,512]{2,1,0:T(8,128)(2,1)} async-done(((bf16[4,256,1024]{2,1,0:T(8,128)(2,1)}), bf16[4,256,512]{2,1,0:T(8,128)(2,1)}) %reduce-scatter.4.cloned.1.call-update) | async-done | bytes 1048592 | tf_op jit(solution)/shard_map/reduce_scatter | solution.py:142
  113.9 1.8 convert_reduce_fusion
  115.7 2.5 %all-reduce = (f32[4,256]{1,0:T(4,128)S(1)}, f32[4,256]{1,0:T(4,128)S(1)}) all-reduce(f32[4,256]{1,0:T(4,128)S(1)} %get-tuple-element.3, f32[4,256]{1,0:T(4,128)S(1)} %get-tuple-element.2), channel_id=1, replica_groups=mesh['tm'=16,'mp'=2] {'mp'}, use_global_device_ids=true, to_apply=%region_12.13 | all-reduce | flops 2048 | bytes 16384 | tf_op jit(solution)/shard_map/psum | solution.py:151
  118.2 1.4 fusion.28
  119.7 1.9 %slice.95 = bf16[4,64,1024]{2,1,0:T(8,128)(2,1)} slice(bf16[4,320,1024]{2,1,0:T(8,128)(2,1)} %copy-done.8), slice={[0:4], [256:320], [0:1024]} | slice | bytes 1048576 | tf_op jit(solution)/shard_map/slice | solution.py:140
  121.6 10.0 %all-gather.6.cloned.1.call-done = bf16[8,256,512]{2,1,0:T(8,128)(2,1)} async-done(((bf16[4,256,512]{2,1,0:T(8,128)(2,1)}), bf16[8,256,512]{2,1,0:T(8,128)(2,1)}) %all-gather.6.cloned.1.call-update) | async-done | bytes 2097168 | tf_op jit(solution)/shard_map/all_gather | solution.py:160
  131.6 5.1 %copy.59 = bf16[2,4,256,512]{3,0,2,1:T(2,128)(2,1)} copy(bf16[2,4,256,512]{3,2,1,0:T(8,128)(2,1)} %bitcast.62) | data formatting | bytes 4194304 | tf_op jit(solution)/shard_map/all_gather | solution.py:160
  136.7 4.4 %dot_general.42 = bf16[4,256,1024]{2,1,0:T(8,128)(2,1)} reshape(bf16[4,256,2,512]{3,2,1,0:T(2,128)(2,1)} %bitcast.61) | data formatting | bytes 4194304 | tf_op jit(solution)/shard_map/dot_general | solution.py:30
  141.1 14.4 %fusion.47 = bf16[4,256,1024]{2,1,0:T(8,128)(2,1)} fusion(bf16[2048,1024]{1,0:T(8,128)(2,1)} %param.25, bf16[4,256,1024]{2,1,0:T(8,128)(2,1)} %dot_general.42, bf16[1024,2048]{1,0:T(8,128)(2,1)} %param.24), kind=kOutput, calls=%fused_computation.58 | convolution fusion | flops 8609857536 | bytes 12582912 | tf_op jit(solution)/shard_map/dot_general | solution.py:30
  155.6 0.1 broadcast_compare_fusion.3
  155.7 1.8 %select_convert_fusion.1 = bf16[4,64,512]{2,1,0:T(8,128)(2,1)} fusion(bf16[4,64,512]{2,1,0:T(8,128)(2,1)} %reduce-scatter.8.cloned.1.call-done, pred[4,64]{1,0:T(4,128)(4,1)S(1)} %broadcast_compare_fusion.3), kind=kLoop, calls=%fused_computation.83 | loop fusion | flops 393216 | bytes 524544 | tf_op jit(solution)/shard_map/convert_element_type | solution.py:168
  157.5 9.1 %reduce-scatter.6.cloned.1.call-done = bf16[4,256,512]{2,1,0:T(8,128)(2,1)} async-done(((bf16[4,256,1024]{2,1,0:T(8,128)(2,1)}), bf16[4,256,512]{2,1,0:T(8,128)(2,1)}) %reduce-scatter.6.cloned.1.call-update) | async-done | bytes 1048592 | tf_op jit(solution)/shard_map/reduce_scatter | solution.py:162
  166.5 2.5 %fusion.31 = bf16[4,256,512]{2,1,0:T(8,128)(2,1)} fusion(bf16[4,256,512]{2,1,0:T(8,128)(2,1)S(1)} %get-tuple-element.6, bf16[4,256,512]{2,1,0:T(8,128)(2,1)} %reduce-scatter.6.cloned.1.call-done, pred[4,256]{1,0:T(4,128)(4,1)S(1)} %broadcast_compare_fusion.2), kind=kLoop, calls=%fused_computation.38 | loop fusion | flops 2621440 | bytes 3146752 | tf_op jit(solution)/shard_map/convert_element_type | solution.py:167
  (89 shorter events, 0.7 us)
Async XLA Ops:
  7.2 91.9 %copy-start = (bf16[512,1024]{1,0:T(8,128)(2,1)S(1)}, bf16[512,1024]{1,0:T(8,128)(2,1)}, u32[]{:S(2)}) copy-start(bf16[512,1024]{1,0:T(8,128)(2,1)} %param.22) | copy-start | bytes 3145732
  7.2 2.4 %copy-start.21 = (s32[4]{0:T(128)S(1)}, s32[4]{0:T(128)}, u32[]{:S(2)}) copy-start(s32[4]{0:T(128)} %param.14) | copy-start | bytes 52
  7.2 18.6 %all-gather.4.cloned.1.call-start = ((), (), s32[]{:S(2)}) async-start(), calls=%async_computation.3 | async-start | bytes 3145728 | tf_op jit(solution)/shard_map/all_gather | solution.py:73
  8.9 3.5 %copy-start.18 = (bf16[4,64,512]{2,1,0:T(8,128)(2,1)S(1)}, bf16[4,64,512]{2,1,0:T(8,128)(2,1)}, u32[]{:S(2)}) copy-start(bf16[4,64,512]{2,1,0:T(8,128)(2,1)} %param.16) | copy-start | bytes 786436
  9.6 5.2 %copy-start.20 = (s32[4,64]{1,0:T(4,128)S(1)}, s32[4,64]{1,0:T(4,128)}, u32[]{:S(2)}) copy-start(s32[4,64]{1,0:T(4,128)} %param.15) | copy-start | bytes 3076
  12.3 101.6 %reduce-scatter.4.cloned.1.call-start = ((), (), s32[]{:S(2)}) async-start(), calls=%async_computation.4 | async-start | bytes 3145728 | tf_op jit(solution)/shard_map/reduce_scatter | solution.py:142
  14.7 11.1 %copy-start.3 = (bf16[4,64,1024]{2,1,0:T(8,128)(2,1)}, bf16[4,64,1024]{2,1,0:T(8,128)(2,1)S(1)}, u32[]{:S(2)}) copy-start(bf16[4,64,1024]{2,1,0:T(8,128)(2,1)S(1)} %all_gather.13) | copy-start | bytes 1572868
  30.6 9.0 %copy-start.1 = (bf16[4,256,1024]{2,1,0:T(8,128)(2,1)S(1)}, bf16[4,256,1024]{2,1,0:T(8,128)(2,1)}, u32[]{:S(2)}) copy-start(bf16[4,256,1024]{2,1,0:T(8,128)(2,1)} %all-gather.4.cloned.1.call-done) | copy-start | bytes 6291460
  37.9 2.7 %copy-start.2 = (f32[4,64,1024]{2,1,0:T(8,128)S(1)}, f32[4,64,1024]{2,1,0:T(8,128)}, u32[]{:S(2)}) copy-start(f32[4,64,1024]{2,1,0:T(8,128)} %reduce_sum.94) | copy-start | bytes 3145732
  37.9 2.7 %copy-start.4 = (bf16[4,64,1024]{2,1,0:T(8,128)(2,1)S(1)}, bf16[4,64,1024]{2,1,0:T(8,128)(2,1)}, u32[]{:S(2)}) copy-start(bf16[4,64,1024]{2,1,0:T(8,128)(2,1)} %copy-done.3) | copy-start | bytes 1572868
  37.9 2.7 %copy-start.19 = (f32[1024]{0:T(1024)S(1)}, f32[1024]{0:T(1024)}, u32[]{:S(2)}) copy-start(f32[1024]{0:T(1024)} %param.18) | copy-start | bytes 12292
  41.0 1.2 copy-start.23
  42.2 1.5 copy-start.24
  43.8 17.1 %copy-start.7 = (bf16[4,320,512]{2,1,0:T(8,128)(2,1)}, bf16[4,320,512]{2,1,0:T(8,128)(2,1)S(1)}, u32[]{:S(2)}) copy-start(bf16[4,320,512]{2,1,0:T(8,128)(2,1)S(1)} %fusion.59) | copy-start | bytes 3932164
  45.4 15.6 %copy-start.6 = (bf16[4,320,512]{2,1,0:T(8,128)(2,1)}, bf16[4,320,512]{2,1,0:T(8,128)(2,1)S(1)}, u32[]{:S(2)}) copy-start(bf16[4,320,512]{2,1,0:T(8,128)(2,1)S(1)} %fusion.60) | copy-start | bytes 3932164
  45.4 12.9 %copy-start.25 = (bf16[1024,512]{1,0:T(8,128)(2,1)S(1)}, bf16[1024,512]{1,0:T(8,128)(2,1)}, u32[]{:S(2)}) copy-start(bf16[1024,512]{1,0:T(8,128)(2,1)} %param.19) | copy-start | bytes 3145732
  45.5 6.6 %copy-start.9 = (bf16[1,4,64,512]{3,2,1,0:T(8,128)(2,1)}, bf16[1,4,64,512]{3,2,1,0:T(8,128)(2,1)S(1)}, u32[]{:S(2)}) copy-start(bf16[1,4,64,512]{3,2,1,0:T(8,128)(2,1)S(1)} %get-tuple-element.22) | copy-start | bytes 786436
  45.5 7.5 %copy-start.11 = (bf16[1,4,64,512]{3,2,1,0:T(8,128)(2,1)}, bf16[1,4,64,512]{3,2,1,0:T(8,128)(2,1)S(1)}, u32[]{:S(2)}) copy-start(bf16[1,4,64,512]{3,2,1,0:T(8,128)(2,1)S(1)} %get-tuple-element.23) | copy-start | bytes 786436
  46.3 23.3 %collective-permute-start = (bf16[2,4,32,512]{3,2,1,0:T(8,128)(2,1)}, bf16[2,4,32,512]{3,2,1,0:T(8,128)(2,1)}, u32[]{:S(2)}, u32[]{:S(2)}) collective-permute-start(bf16[2,4,32,512]{3,2,1,0:T(8,128)(2,1)} %pad_maximum_fusion.8), channel_id=1, source_target_pairs={{0,2},{2,4},{4,6},{6,8},{8,10},{10,12},{12,14},{14,16},{16,18},{18... | collective-permute-start | bytes 786440 | tf_op jit(solution)/shard_map/ppermute | solution.py:18
  50.8 16.6 %collective-permute-start.1 = (bf16[2,4,4,512]{3,2,1,0:T(4,128)(2,1)S(1)}, bf16[2,4,4,512]{3,2,1,0:T(4,128)(2,1)S(1)}, u32[]{:S(2)}, u32[]{:S(2)}) collective-permute-start(bf16[2,4,4,512]{3,2,1,0:T(4,128)(2,1)S(1)} %pad_maximum_fusion.9), channel_id=1, source_target_pairs={{2,0},{4,2},{6,4},{8,6},{10,8},{12,10},{14,12},{16,14},{18,16},{20... | collective-permute-start | bytes 98312 | tf_op jit(solution)/shard_map/ppermute | solution.py:18
  52.9 19.7 %collective-permute-start.2 = (bf16[2,4,64,512]{3,2,1,0:T(8,128)(2,1)}, bf16[2,4,64,512]{3,2,1,0:T(8,128)(2,1)}, u32[]{:S(2)}, u32[]{:S(2)}) collective-permute-start(bf16[2,4,64,512]{3,2,1,0:T(8,128)(2,1)} %pad_maximum_fusion.7), channel_id=1, source_target_pairs={{0,2},{2,4},{4,6},{6,8},{8,10},{10,12},{12,14},{14,16},{16,18},{18... | collective-permute-start | bytes 1572872 | tf_op jit(solution)/shard_map/ppermute | solution.py:18
  60.9 1.2 slice-start.1
  62.1 3.9 %slice-start = ((bf16[4,320,512]{2,1,0:T(8,128)(2,1)}), bf16[4,256,512]{2,1,0:T(8,128)(2,1)S(1)}, s32[]{:S(2)}) async-start(bf16[4,320,512]{2,1,0:T(8,128)(2,1)} %copy-done.6), calls=%async_computation.8 | async-start | bytes 2097152 | tf_op jit(solution)/shard_map/slice | solution.py:93
  66.0 6.6 %copy-start.10 = (bf16[1,4,64,512]{3,2,1,0:T(8,128)(2,1)S(1)}, bf16[1,4,64,512]{3,2,1,0:T(8,128)(2,1)}, u32[]{:S(2)}) copy-start(bf16[1,4,64,512]{3,2,1,0:T(8,128)(2,1)} %copy-done.9) | copy-start | bytes 786436
  66.0 6.6 %copy-start.12 = (bf16[1,4,64,512]{3,2,1,0:T(8,128)(2,1)S(1)}, bf16[1,4,64,512]{3,2,1,0:T(8,128)(2,1)}, u32[]{:S(2)}) copy-start(bf16[1,4,64,512]{3,2,1,0:T(8,128)(2,1)} %copy-done.11) | copy-start | bytes 786436
  73.7 1.4 copy-start.14
  75.1 13.0 %copy-start.13 = (bf16[4,256,512]{1,2,0:T(8,128)(2,1)S(1)}, bf16[4,256,512]{1,2,0:T(8,128)(2,1)}, u32[]{:S(2)}) copy-start(bf16[4,256,512]{1,2,0:T(8,128)(2,1)} %copy.41) | copy-start | bytes 3145732
  75.1 13.0 %copy-start.15 = (pred[4,320,420]{1,2,0:T(8,128)(4,1)S(1)}, pred[4,320,420]{1,2,0:T(8,128)(4,1)}, u32[]{:S(2)}) copy-start(pred[4,320,420]{1,2,0:T(8,128)(4,1)} %pad_add_fusion) | copy-start | bytes 1612804
  75.1 13.0 %copy-start.16 = (bf16[1,4,32,512]{2,3,1,0:T(8,128)(2,1)S(1)}, bf16[1,4,32,512]{2,3,1,0:T(8,128)(2,1)}, u32[]{:S(2)}) copy-start(bf16[1,4,32,512]{2,3,1,0:T(8,128)(2,1)} %copy.54) | copy-start | bytes 393220
  75.1 13.0 %copy-start.17 = (bf16[1,4,4,512]{2,3,1,0:T(8,128)(2,1)S(1)}, bf16[1,4,4,512]{2,3,1,0:T(8,128)(2,1)}, u32[]{:S(2)}) copy-start(bf16[1,4,4,512]{2,3,1,0:T(8,128)(2,1)} %copy.55) | copy-start | bytes 49156
  100.7 1.5 copy-start.8
  102.2 1.8 %copy-start.22 = (f32[1024]{0:T(1024)S(1)}, f32[1024]{0:T(1024)}, u32[]{:S(2)}) copy-start(f32[1024]{0:T(1024)} %param.23) | copy-start | bytes 12292
  102.2 11.8 %copy-start.5 = (bf16[4,256,512]{2,1,0:T(8,128)(2,1)S(1)}, bf16[4,256,512]{2,1,0:T(8,128)(2,1)}, u32[]{:S(2)}) copy-start(bf16[4,256,512]{2,1,0:T(8,128)(2,1)} %select_convert_fusion) | copy-start | bytes 3145732
  103.7 27.9 %all-gather.6.cloned.1.call-start = ((), (), s32[]{:S(2)}) async-start(), calls=%async_computation.7 | async-start | bytes 3145728 | tf_op jit(solution)/shard_map/all_gather | solution.py:160
  119.6 36.1 %reduce-scatter.8.cloned.1.call-start = ((), (), s32[]{:S(2)}) async-start(), calls=%async_computation.6 | async-start | bytes 786432 | tf_op jit(solution)/shard_map/reduce_scatter | solution.py:145
  121.6 45.0 %reduce-scatter.6.cloned.1.call-start = ((), (), s32[]{:S(2)}) async-start(), calls=%async_computation.5 | async-start | bytes 3145728 | tf_op jit(solution)/shard_map/reduce_scatter | solution.py:162
Sparse Core Ops, SparseCore 0:
  12.5 13.2 all-gather.3
  103.8 10.0 reduce-scatter.3
  119.7 11.8 all-gather.5
  133.7 9.0 reduce-scatter.7
  155.7 10.7 reduce-scatter.5
